TPU v7x, 32 devices: a whole 2x2x4 slice. The times are simulated.
32 devices in a mesh: mem: 8 (over z, y), lat: 4 (over x, core).
Axes of the slice: x: 2, y: 2, z: 4, core: 2. Of those that a mesh axis runs over, the one named last changes fastest.
Arguments:
- replica_variables: float32 [8, 4, 64, 4096], P('mem', None, 'lat'), may hold values from -40 to 40, as said below
- analysis: float32 [4, 64, 4096], P(None, 'lat'), may hold values from -4 to 4
- labels: int32 [64, 32], P('lat'), may hold values from 0 to 7, as said below
- pairing: int32 [8], replicated, may hold values from 0 to 7, as said below
Outputs:
- closing_ensemble_values: float32 [8, 4, 64, 4096], P('mem', None, 'lat')
- factor: float32 [8, 8], P('mem')
Inputs may be any that keep to these rules, and one draw needn't show every extreme that they name: `replica_variables`: member fields; the spread of members differs across rows and columns. `labels`: every label value occurs at least once. pairing[pairing[m]] = m and pairing[m] != m for every member m.
All inputs are finite; a program needn't handle non-finite values.
Results may differ from a plain program's by a relative error of at most 0.00015.
Values sent between devices are 32-bit elements; how exact they have to be, the bound alone decides.
A program may use at most 64 MiB of HBM per device.

v0:
```python
import functools

import jax
import numpy as np
import jax.numpy as jnp
from jax import lax
from jax.experimental import pallas as pl
from jax.experimental.pallas import tpu as pltpu
from jax.sharding import PartitionSpec as P

MESH = pl.DeviceIdType.MESH
TILE = 128
REGIONS = 8
STEPS = 3
HALO = 2 * STEPS
VMEM_LIMIT = 24 * 2**20
FIELDS = 4
REACH = (2 * STEPS - 1, 2 * STEPS - 1, 2 * STEPS, STEPS)


grav_coef = 0.1
depth_coef = 0.1
advect_coef = 0.05
diffuse_coef = 0.05
coriolis_coef = 0.05
target_size = 0.5
small_eps = 1e-06


def shift_lon(plane):
    sub = plane.shape[0]
    lane = lax.broadcasted_iota(jnp.int32, plane.shape, 1)
    east = pltpu.roll(plane, TILE - 1, 1)
    east = jnp.where(lane == TILE - 1, pltpu.roll(east, sub - 1, 0), east)
    west = pltpu.roll(plane, 1, 1)
    west = jnp.where(lane == 0, pltpu.roll(west, 1, 0), west)
    return east, west


def diff_lon(plane):
    east, west = shift_lon(plane)
    return east - west


def run_steps(state, buf, spare, local_rows, sub, start, rows_all):
    extent = local_rows + 2 * HALO

    def at(field, e):
        return pl.ds((field * extent + e) * sub, sub)

    def masked(e, plane):
        if HALO <= e < HALO + local_rows:
            return plane
        row = start + (e - HALO)
        return jnp.where((row >= 0) & (row < rows_all), 1.0, 0.0).astype(jnp.float32) * plane

    def coriolis(e):
        row = (start + (e - HALO)).astype(jnp.float32)
        return coriolis_coef * (2.0 * (row + 0.5) / rows_all - 1.0)

    tracer_source, source_field = state, 3
    for step in range(STEPS):
        margin = 2 * (STEPS - 1 - step)
        narrow = STEPS - 1 - step
        target, target_field = (spare, 0) if step % 2 == 0 else (buf, 3)
        own = (HALO, HALO + local_rows)
        for e in range(own[0] - margin - 1, own[1] + margin + 1):
            divergence = diff_lon(state[at(1, e), :]) + state[at(2, e + 1), :] - state[at(2, e - 1), :]
            buf[at(0, e), :] = masked(e, state[at(0, e), :] - depth_coef * divergence)
        for e in range(own[0] - margin, own[1] + margin):
            f = coriolis(e)
            v = state[at(2, e), :]
            u1 = state[at(1, e), :] + f * v - grav_coef * diff_lon(buf[at(0, e), :])
            slope = buf[at(0, e + 1), :] - buf[at(0, e - 1), :]
            buf[at(1, e), :] = u1
            buf[at(2, e), :] = masked(e, v - f * u1 - grav_coef * slope)
        for e in range(own[0] - narrow, own[1] + narrow):
            q = tracer_source[at(source_field, e), :]
            upper = tracer_source[at(source_field, e + 1), :]
            lower = tracer_source[at(source_field, e - 1), :]
            east, west = shift_lon(q)
            advected = buf[at(1, e), :] * (east - west) + buf[at(2, e), :] * (upper - lower)
            spreading = east + west + upper + lower - 4.0 * q
            target[at(target_field, e), :] = masked(e, q - advect_coef * advected + diffuse_coef * spreading)
        state = buf
        tracer_source, source_field = target, target_field
    return [(buf, 0), (buf, 1), (buf, 2), (tracer_source, source_field)]


def steps_kernel(size, local_rows, sub, as_rows, *refs):
    extent = local_rows + 2 * HALO
    if as_rows:
        state_ref, factor_ref, out_ref, factor_out, buf, spare = refs
        factor_out[...] = factor_ref[...]
    else:
        state_ref, out_ref, buf, spare = refs
    lat = lax.axis_index("lat")
    fields = run_steps(state_ref, buf, spare, local_rows, sub, lat * local_rows, local_rows * size)
    for field, (ref, place) in enumerate(fields):
        if not as_rows:
            out_ref[pl.ds(field * local_rows * sub, local_rows * sub), :] = ref[
                pl.ds((place * extent + HALO) * sub, local_rows * sub), :
            ]
            continue
        for row in range(0, local_rows, 8):
            for t in range(sub):
                first = (place * extent + HALO + row) * sub + t
                out_ref[field, row : row + 8, t * TILE : (t + 1) * TILE] = ref[pl.ds(first, 8, stride=sub), :]


def halo_copies(buf, local_rows, sub, lat, size, send_sem, recv_sem):
    extent = local_rows + 2 * HALO
    mem = lax.axis_index("mem")
    copies = []
    for side, peer in ((0, lat - 1), (1, lat + 1)):
        group = []
        for field in range(FIELDS):
            reach = REACH[field]
            source = HALO if side == 0 else HALO + local_rows - reach
            target = HALO + local_rows if side == 0 else HALO - reach
            group.append(
                pltpu.make_async_remote_copy(
                    src_ref=buf.at[pl.ds((field * extent + source) * sub, reach * sub), :],
                    dst_ref=buf.at[pl.ds((field * extent + target) * sub, reach * sub), :],
                    send_sem=send_sem.at[side, field],
                    recv_sem=recv_sem.at[side, field],
                    device_id=(mem, peer),
                    device_id_type=MESH,
                )
            )
        copies.append(group)
    return copies


def clear_outside(buf, local_rows, sub, lat, size):
    extent = local_rows + 2 * HALO
    zeros = jnp.zeros((HALO * sub, TILE), jnp.float32)

    @pl.when(lat == 0)
    def _():
        for field in range(FIELDS):
            buf[pl.ds(field * extent * sub, HALO * sub), :] = zeros

    @pl.when(lat == size - 1)
    def _():
        for field in range(FIELDS):
            buf[pl.ds((field * extent + HALO + local_rows) * sub, HALO * sub), :] = zeros


def start_halo(copies, lat, size):
    for side, has in ((0, lat > 0), (1, lat < size - 1)):

        @pl.when(has)
        def _(side=side):
            for copy in copies[side]:
                copy.start()


def finish_halo(copies, lat, size):
    for side, has in ((0, lat > 0), (1, lat < size - 1)):

        @pl.when(has)
        def _(side=side):
            for copy in copies[side]:
                copy.wait_send()
            for copy in copies[1 - side]:
                copy.wait_recv()


def planes_from_rows(source, buf, local_rows, sub):
    extent = local_rows + 2 * HALO
    for field in range(FIELDS):
        for row in range(0, local_rows, 8):
            for t in range(sub):
                first = (field * extent + HALO + row) * sub + t
                buf[pl.ds(first, 8, stride=sub), :] = source[field, row : row + 8, t * TILE : (t + 1) * TILE]


def first_kernel(size, local_rows, sub, x_ref, lab_ref, buf, edge_ref, send_sem, recv_sem, lab_send, lab_recv):
    lat = lax.axis_index("lat")
    mem = lax.axis_index("mem")
    barrier = pltpu.get_barrier_semaphore()
    for peer, has in ((lat - 1, lat > 0), (lat + 1, lat < size - 1)):

        @pl.when(has)
        def _(peer=peer):
            pl.semaphore_signal(barrier, inc=1, device_id=(mem, peer), device_id_type=MESH)

    clear_outside(buf, local_rows, sub, lat, size)
    planes_from_rows(x_ref, buf, local_rows, sub)
    none = jnp.full((sub, TILE), -1.0, jnp.float32)

    @pl.when(lat == 0)
    def _():
        edge_ref[0] = none

    @pl.when(lat == size - 1)
    def _():
        edge_ref[1] = none

    inner = (lat > 0) & (lat < size - 1)

    @pl.when(inner)
    def _():
        pl.semaphore_wait(barrier, 2)

    @pl.when(jnp.logical_not(inner))
    def _():
        pl.semaphore_wait(barrier, 1)

    copies = halo_copies(buf, local_rows, sub, lat, size, send_sem, recv_sem)
    for side, peer in ((0, lat - 1), (1, lat + 1)):
        row = 0 if side == 0 else local_rows - 1
        copies[side].append(
            pltpu.make_async_remote_copy(
                src_ref=lab_ref.at[row],
                dst_ref=edge_ref.at[1 - side],
                send_sem=lab_send.at[side],
                recv_sem=lab_recv.at[side],
                device_id=(mem, peer),
                device_id_type=MESH,
            )
        )
    start_halo(copies, lat, size)
    finish_halo(copies, lat, size)


def second_kernel(
    size, local_rows, sub, first_ref, partner_ref, analysis_ref, lab_ref, edge_ref, buf, factor_ref,
    spread, sums, send_sem, recv_sem, sum_send, sum_recv,
):
    lat = lax.axis_index("lat")
    mem = lax.axis_index("mem")
    extent = local_rows + 2 * HALO
    barrier = pltpu.get_barrier_semaphore()
    for hop in range(1, size):
        pl.semaphore_signal(barrier, inc=1, device_id=(mem, lax.rem(lat + hop, size)), device_id_type=MESH)

    def fold(plane):
        total = plane[0:8]
        for i in range(8, sub, 8):
            total = total + plane[i : i + 8]
        return total

    energies = [jnp.zeros((8, TILE), jnp.float32) for _ in range(REGIONS)]
    counts = [jnp.zeros((8, TILE), jnp.float32) for _ in range(REGIONS)]

    def accumulate(row, carry):
        energies, counts = carry
        total = jnp.zeros((sub, TILE), jnp.float32)
        for field in range(FIELDS):
            place = pl.ds(pl.multiple_of((field * local_rows + row) * sub, sub), sub)
            half = 0.5 * (first_ref[place, :] - partner_ref[place, :])
            spread[field, row] = half
            total = total + half * half
        quarter = 0.125 * total
        here = lab_ref[row]
        before = jnp.where(row == 0, edge_ref[0], lab_ref[jnp.maximum(row - 1, 0)])
        after = jnp.where(row == local_rows - 1, edge_ref[1], lab_ref[jnp.minimum(row + 1, local_rows - 1)])
        new_energies, new_counts = [], []
        for k in range(REGIONS):
            kept = jnp.where(here == k, 1.0, 0.0)
            weight = 2.0 * kept + jnp.where(before == k, 1.0, 0.0) + jnp.where(after == k, 1.0, 0.0)
            new_energies.append(energies[k] + fold(quarter * weight))
            new_counts.append(counts[k] + fold(kept))
        return new_energies, new_counts

    energies, counts = lax.fori_loop(0, local_rows, accumulate, (energies, counts))
    for k in range(REGIONS):
        sums[0, k : k + 1, :] = jnp.sum(energies[k], axis=0, keepdims=True)
        sums[0, REGIONS + k : REGIONS + k + 1, :] = jnp.sum(counts[k], axis=0, keepdims=True)

    pl.semaphore_wait(barrier, size - 1)
    sends = []
    for hop in range(1, size):
        sends.append(
            pltpu.make_async_remote_copy(
                src_ref=sums.at[0],
                dst_ref=sums.at[hop],
                send_sem=sum_send.at[hop],
                recv_sem=sum_recv.at[hop],
                device_id=(mem, lax.rem(lat + hop, size)),
                device_id_type=MESH,
            )
        )
    for copy in sends:
        copy.start()
    clear_outside(buf, local_rows, sub, lat, size)
    planes_from_rows(analysis_ref, buf, local_rows, sub)
    for copy in sends:
        copy.wait()
    total = sums[0]
    for hop in range(1, size):
        total = total + sums[hop]
    total = jnp.sum(total, axis=1, keepdims=True)
    factor = target_size / jnp.sqrt(total[:REGIONS] / total[REGIONS:] + small_eps)
    wide = jnp.broadcast_to(factor, (REGIONS, TILE))
    diagonal = lax.broadcasted_iota(jnp.int32, (REGIONS, TILE), 0) == lax.broadcasted_iota(
        jnp.int32, (REGIONS, TILE), 1
    )
    factor_ref[...] = jnp.sum(jnp.where(diagonal, wide, 0.0), axis=0, keepdims=True)[:, :REGIONS]
    lanes = [jnp.broadcast_to(wide[k : k + 1], (sub, TILE)) for k in range(REGIONS)]

    def middle(row, carry):
        here = lab_ref[row]
        scale = lanes[0]
        for k in range(1, REGIONS):
            scale = jnp.where(here == k, lanes[k], scale)
        for field in range(FIELDS):
            place = pl.ds(pl.multiple_of((field * extent + HALO + row) * sub, sub), sub)
            buf[place, :] = buf[place, :] + scale * spread[field, row]
        return carry

    lax.fori_loop(0, local_rows, middle, 0)
    copies = halo_copies(buf, local_rows, sub, lat, size, send_sem, recv_sem)
    start_halo(copies, lat, size)
    finish_halo(copies, lat, size)


def matchings(items):
    if not items:
        return [[]]
    first, rest = items[0], items[1:]
    return [
        [(first, other)] + tail
        for i, other in enumerate(rest)
        for tail in matchings(rest[:i] + rest[i + 1 :])
    ]


def matchings_count(size):
    count = 1
    for i in range(size - 1, 0, -2):
        count *= i
    return count


def partner_fields(fields, pairing):
    size = lax.axis_size("mem")
    if matchings_count(size) > 512:
        piece = lax.all_gather(fields, "mem", axis=0)
        partner_index = pairing[lax.axis_index("mem")]
        return lax.dynamic_index_in_dim(piece, partner_index, 0, keepdims=False)
    perms = [
        [(i, j) for i, j in match] + [(j, i) for i, j in match]
        for match in matchings(list(range(size)))
    ]
    table = np.zeros((len(perms), size), np.int32)
    for row, perm in enumerate(perms):
        for i, j in perm:
            table[row, i] = j
    hits = jnp.all(jnp.asarray(table) == pairing[None], axis=1)
    index = jnp.sum(jnp.where(hits, jnp.arange(len(perms), dtype=jnp.int32), 0))
    branches = [functools.partial(lax.ppermute, axis_name="mem", perm=perm) for perm in perms]
    return lax.switch(index, branches, fields)


def recentre(spread, centre_fields, region_sum, cells, onehot):
    factor = target_size / jnp.sqrt(region_sum / cells + small_eps)
    cell_factor = jnp.einsum("mk,rtk->mrt", factor, onehot, precision=lax.Precision.HIGHEST)
    members, fields_count, local_rows, width = spread.shape
    scaled = (
        spread.reshape(members, fields_count, local_rows, width // TILE, TILE)
        * cell_factor[:, None, :, :, None]
    ).reshape(spread.shape)
    return (centre_fields[None] + scaled, factor)


def local(replica_variables, analysis, labels, pairing):
    size = lax.axis_size("lat")
    fields, local_rows, width = analysis.shape
    sub = width // TILE
    extent = local_rows + 2 * HALO
    planes = jax.ShapeDtypeStruct((fields * local_rows * sub, TILE), jnp.float32)
    extended = jax.ShapeDtypeStruct((fields * extent * sub, TILE), jnp.float32)
    edges = jax.ShapeDtypeStruct((2, sub, TILE), jnp.float32)
    factors = jax.ShapeDtypeStruct((1, REGIONS), jnp.float32)
    label_planes = jnp.broadcast_to(labels.astype(jnp.float32)[..., None], (local_rows, sub, TILE))
    whole = pl.BlockSpec(memory_space=pltpu.VMEM)
    buffers = [
        pltpu.VMEM((fields * extent * sub, TILE), jnp.float32),
        pltpu.VMEM((extent * sub, TILE), jnp.float32),
    ]
    halo_sems = [pltpu.SemaphoreType.DMA((2, fields)), pltpu.SemaphoreType.DMA((2, fields))]
    state, edge = pl.pallas_call(
        functools.partial(first_kernel, size, local_rows, sub),
        out_shape=(extended, edges),
        in_specs=[whole] * 2,
        out_specs=(whole, whole),
        scratch_shapes=halo_sems + [pltpu.SemaphoreType.DMA((2,)), pltpu.SemaphoreType.DMA((2,))],
        compiler_params=pltpu.CompilerParams(collective_id=0, has_side_effects=True, vmem_limit_bytes=VMEM_LIMIT),
    )(replica_variables[0], label_planes)
    first = pl.pallas_call(
        functools.partial(steps_kernel, size, local_rows, sub, False),
        out_shape=planes,
        in_specs=[whole],
        out_specs=whole,
        scratch_shapes=buffers,
        compiler_params=pltpu.CompilerParams(vmem_limit_bytes=VMEM_LIMIT),
    )(state)
    partner = partner_fields(first, pairing)
    state, factor = pl.pallas_call(
        functools.partial(second_kernel, size, local_rows, sub),
        out_shape=(extended, factors),
        in_specs=[whole] * 5,
        out_specs=(whole, whole),
        scratch_shapes=[
            pltpu.VMEM((fields, local_rows, sub, TILE), jnp.float32),
            pltpu.VMEM((size, 2 * REGIONS, TILE), jnp.float32),
        ]
        + halo_sems
        + [pltpu.SemaphoreType.DMA((size,)), pltpu.SemaphoreType.DMA((size,))],
        compiler_params=pltpu.CompilerParams(collective_id=1, has_side_effects=True, vmem_limit_bytes=VMEM_LIMIT),
    )(first, partner, analysis, label_planes, edge)
    closing, factor = pl.pallas_call(
        functools.partial(steps_kernel, size, local_rows, sub, True),
        out_shape=(jax.ShapeDtypeStruct(analysis.shape, jnp.float32), factors),
        in_specs=[whole] * 2,
        out_specs=(whole, whole),
        scratch_shapes=buffers,
        compiler_params=pltpu.CompilerParams(vmem_limit_bytes=VMEM_LIMIT),
    )(state, factor)
    return (closing[None], factor)


def solution(mesh):
    return jax.shard_map(
        local,
        mesh=mesh,
        in_specs=(P("mem", None, "lat", None), P(None, "lat", None), P("lat", None), P()),
        out_specs=(P("mem", None, "lat", None), P("mem", None)),
        check_vma=False,
    )
```

profile of v0, /device:TPU:1, one launch (start us, length us, event | category | flops | bytes accessed | tf_op | source)
XLA Modules:
  0.0 91.6 jit_solution(7816004348325395036)
XLA Ops:
  0.6 0.8 compare_reduce_fusion
  1.4 0.6 select_reduce_fusion
  2.7 0.7 convert_element_type.3
  3.4 0.1 broadcast_in_dim.14.lab_ref
  3.5 0.0 copy-start
  3.5 1.2 %copy-done = f32[1,4,16,4096]{3,2,1,0:T(8,128)S(1)} copy-done((f32[1,4,16,4096]{3,2,1,0:T(8,128)S(1)}, f32[1,4,16,4096]{3,2,1,0:T(8,128)}, u32[]{:S(2)}) %copy-start) | copy-done | bytes 1048600
  4.8 14.1 %shard_map.68 = (f32[3584,128]{1,0:T(8,128)S(1)}, f32[2,32,128]{2,1,0:T(8,128)S(1)}) custom-call(f32[4,16,4096]{2,1,0:T(8,128)S(1)} %bitcast.2, f32[16,32,128]{2,1,0:T(8,128)S(1)} %broadcast_in_dim.14.lab_ref), custom_call_target="tpu_custom_call" | custom-call | tf_op jit(solution)/shard_map/pallas_call | solution.py:385
  18.9 0.0 copy-start.1
  18.9 1.8 %shard_map.69.first_ref = f32[2048,128]{1,0:T(8,128)S(1)} custom-call(f32[3584,128]{1,0:T(8,128)S(1)} %get-tuple-element.219.refs_0_), custom_call_target="tpu_custom_call" | custom-call | tf_op jit(solution)/shard_map/pallas_call | solution.py:393
  20.7 32.8 %conditional.1 = (f32[2048,128]{1,0:T(8,128)}) conditional(s32[]{:T(128)} %clamp.3, f32[2048,128]{1,0:T(8,128)S(1)} %shard_map.69.first_ref, f32[2048,128]{1,0:T(8,128)S(1)} %shard_map.69.first_ref, f32[2048,128]{1,0:T(8,128)S(1)} %shard_map.69.first_ref, f32[2048,128]{1,0:T(8,128)S(1)} %shard_map.69.first_ref, ...), branch_computations={%region_2.3_spmd, %region_3.4_spmd, %region_4.5_spmd, %region_5.6_... | conditional | bytes 4194352 | solution.py:355
  20.7 5.3 %collective-permute-start.93 = (f32[2048,128]{1,0:T(8,128)S(1)}, f32[2048,128]{1,0:T(8,128)}, u32[]{:S(2)}, u32[]{:S(2)}) collective-permute-start(f32[2048,128]{1,0:T(8,128)S(1)} %param.93), channel_id=1, source_target_pairs={{0,28},{4,12},{8,16},{20,24},{28,0},{12,4},{16,8},{24,20},{1,29},{... | collective-permute-start | bytes 3145736 | tf_op jit(solution)/shard_map/cond/branch_93_fun/ppermute | solution.py:355
  26.1 27.4 %collective-permute-done.93 = f32[2048,128]{1,0:T(8,128)} collective-permute-done((f32[2048,128]{1,0:T(8,128)S(1)}, f32[2048,128]{1,0:T(8,128)}, u32[]{:S(2)}, u32[]{:S(2)}) %collective-permute-start.93) | collective-permute-done | bytes 1048608 | tf_op jit(solution)/shard_map/cond/branch_93_fun/ppermute | solution.py:355
  53.5 0.0 copy-done.1
  53.5 34.7 %shard_map.70 = (f32[3584,128]{1,0:T(8,128)S(1)}, f32[1,8]{1,0:T(1,128)S(1)}) custom-call(f32[2048,128]{1,0:T(8,128)S(1)} %shard_map.69.first_ref, f32[2048,128]{1,0:T(8,128)} %get-tuple-element.225.partner_ref, f32[4,16,4096]{2,1,0:T(8,128)S(1)} %copy-done.1, f32[16,32,128]{2,1,0:T(8,128)S(1)} %broadcast_in_dim.14.lab_ref, ...), custom_call_target="tpu_custom_call" | custom-call | tf_op jit(solution)/shard_map/pallas_call | solution.py:402
  88.2 3.4 %shard_map.71 = (f32[4,16,4096]{2,1,0:T(8,128)}, f32[1,8]{1,0:T(1,128)}) custom-call(f32[3584,128]{1,0:T(8,128)S(1)} %get-tuple-element.221.refs_0_, f32[1,8]{1,0:T(1,128)S(1)} %get-tuple-element.222.refs_1_), custom_call_target="tpu_custom_call" | custom-call | tf_op jit(solution)/shard_map/pallas_call | solution.py:415
Async XLA Ops:
  3.5 1.2 %copy-start = (f32[1,4,16,4096]{3,2,1,0:T(8,128)S(1)}, f32[1,4,16,4096]{3,2,1,0:T(8,128)}, u32[]{:S(2)}) copy-start(f32[1,4,16,4096]{3,2,1,0:T(8,128)} %param.110) | copy-start | bytes 3145732
  18.9 34.6 %copy-start.1 = (f32[4,16,4096]{2,1,0:T(8,128)S(1)}, f32[4,16,4096]{2,1,0:T(8,128)}, u32[]{:S(2)}) copy-start(f32[4,16,4096]{2,1,0:T(8,128)} %analysis_ref.1) | copy-start | bytes 3145732
  20.7 32.7 %collective-permute-start.93 = (f32[2048,128]{1,0:T(8,128)S(1)}, f32[2048,128]{1,0:T(8,128)}, u32[]{:S(2)}, u32[]{:S(2)}) collective-permute-start(f32[2048,128]{1,0:T(8,128)S(1)} %param.93), channel_id=1, source_target_pairs={{0,28},{4,12},{8,16},{20,24},{28,0},{12,4},{16,8},{24,20},{1,29},{... | collective-permute-start | bytes 3145736 | tf_op jit(solution)/shard_map/cond/branch_93_fun/ppermute | solution.py:355
where the time goes:
time: 92.3 us; the launch traced here: 91.6 us
  Pallas kernels  54 us (59%)
  waiting for transfers between devices  27.4 us (30%)
  starting transfers between devices  5.33 us (6%)
  other arithmetic  2.12 us (2%)
  local copies, waits for them, and re-layouts  1.35 us (1%)
  between operations  1.33 us (1%)
    pallas_call x1, Pallas kernels, local(): pl.pallas_call(functools.partial(second_kernel, size, local_rows, sub), o...  34.7 us
    ppermute x1, waiting for transfers between devices, partner_fields(): return lax.switch(index, branches, fields)  27.4 us
    pallas_call x1, Pallas kernels, local(): pl.pallas_call(functools.partial(first_kernel, size, local_rows, sub), ou...  14.1 us
    ppermute x1, starting transfers between devices, partner_fields(): return lax.switch(index, branches, fields)  5.33 us
    pallas_call x1, Pallas kernels, local(): pl.pallas_call(functools.partial(steps_kernel, size, local_rows, sub, Tru...  3.4 us
  transfers between devices with their start and end apart: 1, of which 1 were waited for; matrix products, arithmetic and copies ran while one was open for 0% of the time, Pallas kernels for 0%

commit v1 on v0

--- a/solution.py
+++ b/solution.py
@@ -1,7 +1,6 @@
 import functools
 
 import jax
-import numpy as np
 import jax.numpy as jnp
 from jax import lax
 from jax.experimental import pallas as pl
@@ -87,20 +86,55 @@
     return [(buf, 0), (buf, 1), (buf, 2), (tracer_source, source_field)]
 
 
+def matchings(items):
+    if not items:
+        return [[]]
+    first, rest = items[0], items[1:]
+    return [
+        [(first, other)] + tail
+        for i, other in enumerate(rest)
+        for tail in matchings(rest[:i] + rest[i + 1 :])
+    ]
+
+
+def permutations(size):
+    count = 1
+    for i in range(size - 1, 0, -2):
+        count *= i
+    if count > 512:
+        return []
+    return [[(i, j) for i, j in m] + [(j, i) for i, j in m] for m in matchings(list(range(size)))]
+
+
+def matching_index(pairing_ref):
+    size = pairing_ref.shape[0]
+    key = 0
+    for i in range(size):
+        key = key * size + pairing_ref[i]
+    index = jnp.int32(0)
+    for branch, perm in enumerate(permutations(size)):
+        known = 0
+        for _, j in sorted(perm):
+            known = known * size + j
+        index = jnp.where(key == known, branch, index)
+    return index
+
+
 def steps_kernel(size, local_rows, sub, as_rows, *refs):
     extent = local_rows + 2 * HALO
     if as_rows:
         state_ref, factor_ref, out_ref, factor_out, buf, spare = refs
         factor_out[...] = factor_ref[...]
     else:
-        state_ref, out_ref, buf, spare = refs
+        state_ref, pairing_ref, out_ref, index_ref, buf, spare = refs
+        index_ref[0, 0] = matching_index(pairing_ref)
     lat = lax.axis_index("lat")
     fields = run_steps(state_ref, buf, spare, local_rows, sub, lat * local_rows, local_rows * size)
     for field, (ref, place) in enumerate(fields):
         if not as_rows:
-            out_ref[pl.ds(field * local_rows * sub, local_rows * sub), :] = ref[
-                pl.ds((place * extent + HALO) * sub, local_rows * sub), :
-            ]
+            for tile in range(local_rows * sub // 8):
+                column = (field * local_rows * sub // 8 + tile) * TILE
+                out_ref[:, column : column + TILE] = ref[pl.ds((place * extent + HALO) * sub + tile * 8, 8), :]
             continue
         for row in range(0, local_rows, 8):
             for t in range(sub):
@@ -167,16 +201,16 @@
                 copy.wait_recv()
 
 
-def planes_from_rows(source, buf, local_rows, sub):
-    extent = local_rows + 2 * HALO
-    for field in range(FIELDS):
+def planes_from_rows(source, buf, local_rows, sub, fields=range(FIELDS)):
+    extent = local_rows + 2 * HALO
+    for field in fields:
         for row in range(0, local_rows, 8):
             for t in range(sub):
                 first = (field * extent + HALO + row) * sub + t
                 buf[pl.ds(first, 8, stride=sub), :] = source[field, row : row + 8, t * TILE : (t + 1) * TILE]
 
 
-def first_kernel(size, local_rows, sub, x_ref, lab_ref, buf, edge_ref, send_sem, recv_sem, lab_send, lab_recv):
+def first_kernel(size, local_rows, sub, x_ref, lab_ref, buf, edge_ref, rows, load_sem, send_sem, recv_sem, lab_send, lab_recv):
     lat = lax.axis_index("lat")
     mem = lax.axis_index("mem")
     barrier = pltpu.get_barrier_semaphore()
@@ -186,8 +220,10 @@
         def _(peer=peer):
             pl.semaphore_signal(barrier, inc=1, device_id=(mem, peer), device_id_type=MESH)
 
+    loads = [pltpu.make_async_copy(x_ref.at[f], rows.at[f], load_sem.at[f]) for f in range(FIELDS)]
+    for load in loads:
+        load.start()
     clear_outside(buf, local_rows, sub, lat, size)
-    planes_from_rows(x_ref, buf, local_rows, sub)
     none = jnp.full((sub, TILE), -1.0, jnp.float32)
 
     @pl.when(lat == 0)
@@ -221,7 +257,11 @@
                 device_id_type=MESH,
             )
         )
-    start_halo(copies, lat, size)
+    for field in range(FIELDS + 1):
+        if field < FIELDS:
+            loads[field].wait()
+            planes_from_rows(rows, buf, local_rows, sub, (field,))
+        start_halo([side[field : field + 1] for side in copies], lat, size)
     finish_halo(copies, lat, size)
 
 
@@ -249,8 +289,12 @@
         energies, counts = carry
         total = jnp.zeros((sub, TILE), jnp.float32)
         for field in range(FIELDS):
-            place = pl.ds(pl.multiple_of((field * local_rows + row) * sub, sub), sub)
-            half = 0.5 * (first_ref[place, :] - partner_ref[place, :])
+            parts = []
+            for i in range(sub // 8):
+                column = ((field * local_rows + row) * (sub // 8) + i) * TILE
+                place = pl.ds(pl.multiple_of(column, TILE), TILE)
+                parts.append(first_ref[:, place] - partner_ref[:, place])
+            half = 0.5 * jnp.concatenate(parts, axis=0)
             spread[field, row] = half
             total = total + half * half
         quarter = 0.125 * total
@@ -317,53 +361,14 @@
     finish_halo(copies, lat, size)
 
 
-def matchings(items):
-    if not items:
-        return [[]]
-    first, rest = items[0], items[1:]
-    return [
-        [(first, other)] + tail
-        for i, other in enumerate(rest)
-        for tail in matchings(rest[:i] + rest[i + 1 :])
-    ]
-
-
-def matchings_count(size):
-    count = 1
-    for i in range(size - 1, 0, -2):
-        count *= i
-    return count
-
-
-def partner_fields(fields, pairing):
+def partner_fields(fields, pairing, index):
     size = lax.axis_size("mem")
-    if matchings_count(size) > 512:
+    perms = permutations(size)
+    if not perms:
         piece = lax.all_gather(fields, "mem", axis=0)
-        partner_index = pairing[lax.axis_index("mem")]
-        return lax.dynamic_index_in_dim(piece, partner_index, 0, keepdims=False)
-    perms = [
-        [(i, j) for i, j in match] + [(j, i) for i, j in match]
-        for match in matchings(list(range(size)))
-    ]
-    table = np.zeros((len(perms), size), np.int32)
-    for row, perm in enumerate(perms):
-        for i, j in perm:
-            table[row, i] = j
-    hits = jnp.all(jnp.asarray(table) == pairing[None], axis=1)
-    index = jnp.sum(jnp.where(hits, jnp.arange(len(perms), dtype=jnp.int32), 0))
+        return lax.dynamic_index_in_dim(piece, pairing[lax.axis_index("mem")], 0, keepdims=False)
     branches = [functools.partial(lax.ppermute, axis_name="mem", perm=perm) for perm in perms]
     return lax.switch(index, branches, fields)
-
-
-def recentre(spread, centre_fields, region_sum, cells, onehot):
-    factor = target_size / jnp.sqrt(region_sum / cells + small_eps)
-    cell_factor = jnp.einsum("mk,rtk->mrt", factor, onehot, precision=lax.Precision.HIGHEST)
-    members, fields_count, local_rows, width = spread.shape
-    scaled = (
-        spread.reshape(members, fields_count, local_rows, width // TILE, TILE)
-        * cell_factor[:, None, :, :, None]
-    ).reshape(spread.shape)
-    return (centre_fields[None] + scaled, factor)
 
 
 def local(replica_variables, analysis, labels, pairing):
@@ -371,7 +376,7 @@
     fields, local_rows, width = analysis.shape
     sub = width // TILE
     extent = local_rows + 2 * HALO
-    planes = jax.ShapeDtypeStruct((fields * local_rows * sub, TILE), jnp.float32)
+    wide = jax.ShapeDtypeStruct((8, fields * local_rows * width // 8), jnp.float32)
     extended = jax.ShapeDtypeStruct((fields * extent * sub, TILE), jnp.float32)
     edges = jax.ShapeDtypeStruct((2, sub, TILE), jnp.float32)
     factors = jax.ShapeDtypeStruct((1, REGIONS), jnp.float32)
@@ -385,20 +390,23 @@
     state, edge = pl.pallas_call(
         functools.partial(first_kernel, size, local_rows, sub),
         out_shape=(extended, edges),
-        in_specs=[whole] * 2,
+        in_specs=[pl.BlockSpec(memory_space=pltpu.HBM), whole],
         out_specs=(whole, whole),
-        scratch_shapes=halo_sems + [pltpu.SemaphoreType.DMA((2,)), pltpu.SemaphoreType.DMA((2,))],
+        scratch_shapes=[pltpu.VMEM(analysis.shape, jnp.float32), pltpu.SemaphoreType.DMA((fields,))]
+        + halo_sems
+        + [pltpu.SemaphoreType.DMA((2,)), pltpu.SemaphoreType.DMA((2,))],
         compiler_params=pltpu.CompilerParams(collective_id=0, has_side_effects=True, vmem_limit_bytes=VMEM_LIMIT),
     )(replica_variables[0], label_planes)
-    first = pl.pallas_call(
+    smem = pl.BlockSpec(memory_space=pltpu.SMEM)
+    first, index = pl.pallas_call(
         functools.partial(steps_kernel, size, local_rows, sub, False),
-        out_shape=planes,
-        in_specs=[whole],
-        out_specs=whole,
+        out_shape=(wide, jax.ShapeDtypeStruct((1, 1), jnp.int32)),
+        in_specs=[whole, smem],
+        out_specs=(whole, smem),
         scratch_shapes=buffers,
         compiler_params=pltpu.CompilerParams(vmem_limit_bytes=VMEM_LIMIT),
-    )(state)
-    partner = partner_fields(first, pairing)
+    )(state, pairing)
+    partner = partner_fields(first, pairing, index[0, 0])
     state, factor = pl.pallas_call(
         functools.partial(second_kernel, size, local_rows, sub),
         out_shape=(extended, factors),

time: 92.3 us -> 93.7 us (1.015)
  Pallas kernels: 54 us -> 55.6 us
  other arithmetic: 2.12 us -> 0.7 us
    pallas_call x1, Pallas kernels: 1.76 us -> 2.82 us  [local(): pl.pallas_call(functools.partial(steps_kernel, size, local_rows, sub, Fal...]
    unnamed x4 -> x6, local copies, waits for them, and re-layouts: 1.23 us -> 1.88 us
where the time goes in v1:
time: 93.7 us; the launch traced here: 93 us
  Pallas kernels  55.6 us (59%)
  waiting for transfers between devices  27.4 us (29%)
  starting transfers between devices  5.81 us (6%)
  local copies, waits for them, and re-layouts  2 us (2%)
  between operations  1.33 us (1%)
    pallas_call x1, Pallas kernels, local(): pl.pallas_call(functools.partial(second_kernel, size, local_rows, sub), o...  35.6 us
    ppermute x1, waiting for transfers between devices, partner_fields(): return lax.switch(index, branches, fields)  27.4 us
    pallas_call x1, Pallas kernels, local(): pl.pallas_call(functools.partial(first_kernel, size, local_rows, sub), ou...  13.8 us
    ppermute x1, starting transfers between devices, partner_fields(): return lax.switch(index, branches, fields)  5.81 us
    pallas_call x1, Pallas kernels, local(): pl.pallas_call(functools.partial(steps_kernel, size, local_rows, sub, Tru...  3.4 us
    pallas_call x1, Pallas kernels, local(): pl.pallas_call(functools.partial(steps_kernel, size, local_rows, sub, Fal...  2.82 us
    unnamed x6, local copies, waits for them, and re-layouts  1.88 us
  transfers between devices with their start and end apart: 1, of which 1 were waited for; matrix products, arithmetic and copies ran while one was open for 0% of the time, Pallas kernels for 0%

profile of v1, /device:TPU:1, one launch (start us, length us, event | category | flops | bytes accessed | tf_op | source)
XLA Modules:
  0.0 93.0 jit_solution(18046975707712988449)
XLA Ops:
  0.6 0.7 convert_element_type.3
  1.3 0.1 broadcast_in_dim.4.lab_ref
  1.5 0.0 copy-start
  1.5 1.2 %copy-done = f32[1,4,16,4096]{3,2,1,0:T(8,128)S(1)} copy-done((f32[1,4,16,4096]{3,2,1,0:T(8,128)S(1)}, f32[1,4,16,4096]{3,2,1,0:T(8,128)}, u32[]{:S(2)}) %copy-start) | copy-done | bytes 1048600
  2.7 0.0 copy-start.1
  2.7 13.8 %shard_map.59 = (f32[3584,128]{1,0:T(8,128)S(1)}, f32[2,32,128]{2,1,0:T(8,128)S(1)}) custom-call(f32[4,16,4096]{2,1,0:T(8,128)S(1)} %bitcast.3, f32[16,32,128]{2,1,0:T(8,128)S(1)} %broadcast_in_dim.4.lab_ref), custom_call_target="tpu_custom_call" | custom-call | tf_op jit(solution)/shard_map/pallas_call | solution.py:390
  16.5 0.0 copy-start.2
  16.6 0.6 copy-done.2
  17.2 2.8 %shard_map.60 = (f32[8,32768]{1,0:T(8,128)S(1)}, s32[1,1]{1,0:T(1,128)}) custom-call(f32[3584,128]{1,0:T(8,128)S(1)} %get-tuple-element.221.refs_0_, s32[8]{0:T(128)S(1)} %copy-done.2), custom_call_target="tpu_custom_call" | custom-call | tf_op jit(solution)/shard_map/pallas_call | solution.py:401
  20.7 33.3 %conditional.1 = (f32[8,32768]{1,0:T(8,128)}) conditional(s32[]{:T(128)} %bitcast.1, f32[8,32768]{1,0:T(8,128)S(1)} %get-tuple-element.222.first_ref, f32[8,32768]{1,0:T(8,128)S(1)} %get-tuple-element.222.first_ref, f32[8,32768]{1,0:T(8,128)S(1)} %get-tuple-element.222.first_ref, ...), branch_computations={%region_0.0_spmd, %region_1.0_spmd, %region_2.0_spmd, %region_3.0_... | conditional | bytes 4194352 | solution.py:371
  20.7 5.8 %collective-permute-start.104 = (f32[8,32768]{1,0:T(8,128)S(1)}, f32[8,32768]{1,0:T(8,128)}, u32[]{:S(2)}, u32[]{:S(2)}) collective-permute-start(f32[8,32768]{1,0:T(8,128)S(1)} %param.104), channel_id=1, source_target_pairs={{0,28},{4,24},{8,20},{12,16},{28,0},{24,4},{20,8},{16,12},{1,29},{... | collective-permute-start | bytes 3145736 | tf_op jit(solution)/shard_map/cond/branch_104_fun/ppermute | solution.py:371
  26.5 27.4 %collective-permute-done.104 = f32[8,32768]{1,0:T(8,128)} collective-permute-done((f32[8,32768]{1,0:T(8,128)S(1)}, f32[8,32768]{1,0:T(8,128)}, u32[]{:S(2)}, u32[]{:S(2)}) %collective-permute-start.104) | collective-permute-done | bytes 1048608 | tf_op jit(solution)/shard_map/cond/branch_104_fun/ppermute | solution.py:371
  54.0 0.0 copy-done.1
  54.0 35.6 %shard_map.61 = (f32[3584,128]{1,0:T(8,128)S(1)}, f32[1,8]{1,0:T(1,128)S(1)}) custom-call(f32[8,32768]{1,0:T(8,128)S(1)} %get-tuple-element.222.first_ref, f32[8,32768]{1,0:T(8,128)} %get-tuple-element.229.partner_ref, f32[4,16,4096]{2,1,0:T(8,128)S(1)} %copy-done.1, f32[16,32,128]{2,1,0:T(8,128)S(1)} %broadcast_in_dim.4.lab_ref, ...), custom_call_target="tpu_custom_call" | custom-call | tf_op jit(solution)/shard_map/pallas_call | solution.py:410
  89.6 3.4 %shard_map.62 = (f32[4,16,4096]{2,1,0:T(8,128)}, f32[1,8]{1,0:T(1,128)}) custom-call(f32[3584,128]{1,0:T(8,128)S(1)} %get-tuple-element.225.refs_0_, f32[1,8]{1,0:T(1,128)S(1)} %get-tuple-element.226.refs_1_), custom_call_target="tpu_custom_call" | custom-call | tf_op jit(solution)/shard_map/pallas_call | solution.py:423
Async XLA Ops:
  1.5 1.2 %copy-start = (f32[1,4,16,4096]{3,2,1,0:T(8,128)S(1)}, f32[1,4,16,4096]{3,2,1,0:T(8,128)}, u32[]{:S(2)}) copy-start(f32[1,4,16,4096]{3,2,1,0:T(8,128)} %param.109) | copy-start | bytes 3145732
  2.7 51.3 %copy-start.1 = (f32[4,16,4096]{2,1,0:T(8,128)S(1)}, f32[4,16,4096]{2,1,0:T(8,128)}, u32[]{:S(2)}) copy-start(f32[4,16,4096]{2,1,0:T(8,128)} %analysis_ref.1) | copy-start | bytes 3145732
  16.5 0.7 copy-start.2
  20.7 33.2 %collective-permute-start.104 = (f32[8,32768]{1,0:T(8,128)S(1)}, f32[8,32768]{1,0:T(8,128)}, u32[]{:S(2)}, u32[]{:S(2)}) collective-permute-start(f32[8,32768]{1,0:T(8,128)S(1)} %param.104), channel_id=1, source_target_pairs={{0,28},{4,24},{8,20},{12,16},{28,0},{24,4},{20,8},{16,12},{1,29},{... | collective-permute-start | bytes 3145736 | tf_op jit(solution)/shard_map/cond/branch_104_fun/ppermute | solution.py:371
